TPU v7x, 128 devices: a whole 4x4x4 slice. The times are simulated.
128 devices in a mesh: row: 8 (over y_hi, x), col: 16 (over y_lo, z, core).
Axes of the slice: x: 4, y: 4 (y_hi: 2, y_lo: 2; y = y_hi * 2 + y_lo), z: 4, core: 2. Of those that a mesh axis runs over, the one named last changes fastest.
Arguments:
- right_side: float32 [16, 512, 512], P('col', 'row'), may hold values from -6 to 6
- affinity_blocks: float32 [16, 16, 8, 128, 128], P('row', 'col'), may hold values from -0.03125 to 0.03125
- block_coords: int32 [16, 16, 8, 2], P('row', 'col'), may hold values from 0 to 3
- block_counts: int32 [16, 16], P('row', 'col'), may hold values from 4 to 8, as said below
Outputs:
- ranking: float32 [16, 512, 512], P('col', 'row')
- residual: float32 [16, 512, 512], P('col', 'row')
Inputs may be any that keep to these rules, and one draw needn't show every extreme that they name: `block_counts`: some grid tile holds 8 live blocks in every draw.
All inputs are finite; a program needn't handle non-finite values.
Results may differ from a plain program's by a relative error of at most 0.0003.
Values sent between devices are 32-bit elements; how exact they have to be, the bound alone decides.
No kernel may reach another device: no remote copies, remote signals or barrier semaphores. Data moves between devices by JAX's collectives and lax.ppermute only.
A program may use at most 64 MiB of HBM per device.

v0:
```python
import jax
import jax.numpy as jnp
from jax import lax
from jax.sharding import PartitionSpec as P

ITERS = 3
diffusion = 0.8


def broadcast(value, axis, source):
    kept = jnp.where(lax.axis_index(axis) == source, value, 0).astype(value.dtype)
    return lax.psum(kept, axis)


def live_blocks(blocks, count):
    live = (jnp.arange(blocks.shape[0], dtype=jnp.int32) < count).astype(blocks.dtype)
    return blocks * live[:, None, None]


def forward_only(masked, rows, cols, column_field):
    position = jnp.arange(column_field.shape[0], dtype=jnp.int32)
    picked = jnp.take(column_field, cols, axis=0)
    product = jnp.einsum("kab,kbw->kaw", masked, picked, precision=lax.Precision.HIGHEST)
    row_onehot = (rows[None, :] == position[:, None]).astype(jnp.float32)
    return jnp.einsum("tk,kaw->taw", row_onehot, product, precision=lax.Precision.HIGHEST)


def backward_only(masked, rows, cols, row_field):
    position = jnp.arange(row_field.shape[0], dtype=jnp.int32)
    chosen = jnp.take(row_field, rows, axis=0)
    mirrored = jnp.einsum("kab,kaw->kbw", masked, chosen, precision=lax.Precision.HIGHEST)
    col_onehot = (cols[None, :] == position[:, None]).astype(jnp.float32)
    return jnp.einsum("tk,kbw->tbw", col_onehot, mirrored, precision=lax.Precision.HIGHEST)


def tile_products(masked, rows, cols, column_field, row_field):
    forward = forward_only(masked, rows, cols, column_field)
    backward = backward_only(masked, rows, cols, row_field)
    return (forward, backward)


def block_products(affinity_blocks, block_coords, block_counts, column_block, row_blocks):
    members = affinity_blocks.shape[0]
    edge = affinity_blocks.shape[-1]
    width = column_block.shape[1]
    column_field = column_block.reshape(-1, edge, width)
    forward_parts = []
    backward_total = jnp.zeros(column_field.shape, jnp.float32)
    for member in range(members):
        masked = live_blocks(affinity_blocks[member, 0], block_counts[member, 0])
        forward, backward = tile_products(
            masked,
            block_coords[member, 0, :, 0],
            block_coords[member, 0, :, 1],
            column_field,
            row_blocks[member].reshape(column_field.shape),
        )
        forward_parts.append(forward.reshape(column_block.shape))
        backward_total = backward_total + backward
    return (jnp.stack(forward_parts), backward_total.reshape(column_block.shape))


def operate(piece, affinity_blocks, block_coords, block_counts):
    rows_count = lax.axis_size("row")
    cols_count = lax.axis_size("col")
    members = cols_count // rows_count
    my_row = lax.axis_index("row")
    share = piece.shape[1]
    width = piece.shape[2]
    sliver = share // cols_count
    whole = lax.all_gather(piece, "row", axis=1, tiled=True)
    received = []
    for member in range(members):
        received.append(broadcast(whole[0], "col", my_row * members + member))
    row_blocks = jnp.stack(received)
    forward, backward = block_products(
        affinity_blocks, block_coords, block_counts, whole[0], row_blocks
    )
    back_part = lax.psum_scatter(backward[None], "row", scatter_dimension=1, tiled=True)
    spread = forward.reshape(members, rows_count, cols_count, sliver, width)
    summed = lax.psum_scatter(spread, "col", scatter_dimension=2, tiled=True)
    ordered = summed.reshape(members, rows_count, sliver, width).transpose(1, 0, 2, 3)
    ordered = ordered.reshape(rows_count * members, sliver, width)
    forward_part = lax.all_to_all(
        lax.all_to_all(ordered, "row", split_axis=0, concat_axis=0, tiled=True),
        "col",
        split_axis=0,
        concat_axis=1,
        tiled=True,
    )
    return piece - diffusion * (forward_part + back_part)


def squares(residual):
    return lax.psum(jnp.sum(residual * residual, axis=(0, 1)), ("row", "col"))


def shards(right_side, affinity_blocks, block_coords, block_counts):
    ranking = jnp.zeros_like(right_side)
    residual = right_side
    direction = right_side
    norm_now = squares(residual)
    for step in range(ITERS):
        image = operate(direction, affinity_blocks, block_coords, block_counts)
        curve = lax.psum(jnp.sum(direction * image, axis=(0, 1)), ("row", "col"))
        alpha = norm_now / curve
        ranking = ranking + alpha * direction
        residual = residual - alpha * image
        if step + 1 < ITERS:
            norm_next = squares(residual)
            direction = residual + norm_next / norm_now * direction
            norm_now = norm_next
    return (ranking, residual)


def solution(mesh):
    in_specs = (
        P("col", "row", None),
        P("row", "col", None, None, None),
        P("row", "col", None, None),
        P("row", "col"),
    )
    out_specs = (P("col", "row", None), P("col", "row", None))
    return jax.shard_map(shards, mesh=mesh, in_specs=in_specs, out_specs=out_specs, check_vma=False)
```

profile of v0, /device:TPU:1, one launch (start us, length us, event | category | flops | bytes accessed | tf_op | source)
XLA Modules:
  0.0 1282.6 jit_solution(11291299337467463532)
XLA Ops:
  9.9 50.0 %all-gather.4.cloned.1.call-done = f32[1,512,512]{2,1,0:T(8,128)} async-done(((f32[1,64,512]{2,1,0:T(8,128)}), f32[1,512,512]{2,1,0:T(8,128)}) %all-gather.4.cloned.1.call-update) | async-done | bytes 1048592 | tf_op jit(solution)/shard_map/all_gather | solution.py:71
  87.5 98.5 %all-reduce.12.cloned.1.call-done = (f32[4,128,512]{2,1,0:T(8,128)}, f32[4,128,512]{2,1,0:T(8,128)}) async-done(((f32[4,128,512]{2,1,0:T(8,128)}, f32[4,128,512]{2,1,0:T(8,128)}), (f32[4,128,512]{2,1,0:T(8,128)}, f32[4,128,512]{2,1,0:T(8,128)})) %all-reduce.12.cloned.1.call-update) | async-done | bytes 2097168 | tf_op jit(solution)/shard_map/psum | solution.py:12
  191.2 3.7 fusion.40
  203.0 46.3 %reduce-scatter.7.cloned.1.call-done = f32[2,8,1,4,512]{4,1,3,0,2:T(8,128)} async-done(((f32[2,8,16,4,512]{4,1,3,0,2:T(8,128)}), f32[2,8,1,4,512]{4,1,3,0,2:T(8,128)}) %reduce-scatter.7.cloned.1.call-update) | async-done | bytes 131088 | tf_op jit(solution)/shard_map/reduce_scatter | solution.py:81
  250.3 13.3 %all_to_all.51 = f32[16,4,512]{2,1,0:T(4,128)S(1)} all-to-all(f32[16,4,512]{2,1,0:T(4,128)S(1)} %bitcast.97), channel_id=1, replica_groups=mesh['row'=8,'col'=16] {'row'}, dimensions={0} | all-to-all | bytes 262144 | tf_op jit(solution)/shard_map/all_to_all | solution.py:85
  263.6 14.2 %all_to_all.52 = f32[16,4,512]{2,1,0:T(4,128)S(1)} all-to-all(f32[16,4,512]{2,1,0:T(4,128)S(1)} %all_to_all.51), channel_id=1, replica_groups=mesh['row'=8,'col'=16] {'col'}, dimensions={0} | all-to-all | bytes 262144 | tf_op jit(solution)/shard_map/all_to_all | solution.py:84
  277.8 47.4 %reduce-scatter.9.cloned.1.call-done = f32[1,64,512]{2,1,0:T(8,128)} async-done(((f32[1,512,512]{2,1,0:T(8,128)}), f32[1,64,512]{2,1,0:T(8,128)}) %reduce-scatter.9.cloned.1.call-update) | async-done | bytes 131088 | tf_op jit(solution)/shard_map/reduce_scatter | solution.py:79
  326.1 66.3 %all-reduce = (f32[512]{0:T(512)S(1)}, f32[512]{0:T(512)S(1)}) all-reduce(f32[512]{0:T(512)S(1)} %get-tuple-element.4, f32[512]{0:T(512)S(1)} %get-tuple-element.3), channel_id=1, replica_groups=mesh['row'=8,'col'=16] {'row','col'}, use_global_device_ids=true, to_apply=%region_1.0 | all-reduce | flops 1024 | bytes 8192 | tf_op jit(solution)/shard_map/psum | solution.py:95
  393.4 62.5 %psum.88 = f32[512]{0:T(512)S(1)} all-reduce(f32[512]{0:T(512)S(1)} %get-tuple-element.15), channel_id=1, replica_groups=mesh['row'=8,'col'=16] {'row','col'}, use_global_device_ids=true, to_apply=%region_9.11 | all-reduce | flops 512 | bytes 4096 | tf_op jit(solution)/shard_map/psum | solution.py:95
  456.7 43.6 %all-gather.6.cloned.1.call-done = f32[1,512,512]{2,1,0:T(8,128)} async-done(((f32[1,64,512]{2,1,0:T(8,128)}), f32[1,512,512]{2,1,0:T(8,128)}) %all-gather.6.cloned.1.call-update) | async-done | bytes 1048592 | tf_op jit(solution)/shard_map/all_gather | solution.py:71
  528.2 98.3 %all-reduce.10.cloned.1.call-done = (f32[4,128,512]{2,1,0:T(8,128)}, f32[4,128,512]{2,1,0:T(8,128)}) async-done(((f32[4,128,512]{2,1,0:T(8,128)}, f32[4,128,512]{2,1,0:T(8,128)}), (f32[4,128,512]{2,1,0:T(8,128)}, f32[4,128,512]{2,1,0:T(8,128)})) %all-reduce.10.cloned.1.call-update) | async-done | bytes 2097168 | tf_op jit(solution)/shard_map/psum | solution.py:12
  643.4 46.4 %reduce-scatter.11.cloned.1.call-done = f32[2,8,1,4,512]{4,1,3,0,2:T(8,128)} async-done(((f32[2,8,16,4,512]{4,1,3,0,2:T(8,128)}), f32[2,8,1,4,512]{4,1,3,0,2:T(8,128)}) %reduce-scatter.11.cloned.1.call-update) | async-done | bytes 131088 | tf_op jit(solution)/shard_map/reduce_scatter | solution.py:81
  690.8 13.3 %all_to_all.53 = f32[16,4,512]{2,1,0:T(4,128)S(1)} all-to-all(f32[16,4,512]{2,1,0:T(4,128)S(1)} %bitcast.98), channel_id=1, replica_groups=mesh['row'=8,'col'=16] {'row'}, dimensions={0} | all-to-all | bytes 262144 | tf_op jit(solution)/shard_map/all_to_all | solution.py:85
  704.1 14.3 %all_to_all.54 = f32[16,4,512]{2,1,0:T(4,128)S(1)} all-to-all(f32[16,4,512]{2,1,0:T(4,128)S(1)} %all_to_all.53), channel_id=1, replica_groups=mesh['row'=8,'col'=16] {'col'}, dimensions={0} | all-to-all | bytes 262144 | tf_op jit(solution)/shard_map/all_to_all | solution.py:84
  718.4 47.8 %reduce-scatter.13.cloned.1.call-done = f32[1,64,512]{2,1,0:T(8,128)} async-done(((f32[1,512,512]{2,1,0:T(8,128)}), f32[1,64,512]{2,1,0:T(8,128)}) %reduce-scatter.13.cloned.1.call-update) | async-done | bytes 131088 | tf_op jit(solution)/shard_map/reduce_scatter | solution.py:79
  767.2 66.3 %psum.91 = f32[512]{0:T(512)S(1)} all-reduce(f32[512]{0:T(512)S(1)} %multiply_reduce_fusion.2), channel_id=1, replica_groups=mesh['row'=8,'col'=16] {'row','col'}, use_global_device_ids=true, to_apply=%region_15.17 | all-reduce | flops 512 | bytes 4096 | tf_op jit(solution)/shard_map/psum | solution.py:105
  834.5 62.5 %psum.92 = f32[512]{0:T(512)S(1)} all-reduce(f32[512]{0:T(512)S(1)} %get-tuple-element.13), channel_id=1, replica_groups=mesh['row'=8,'col'=16] {'row','col'}, use_global_device_ids=true, to_apply=%region_17.19 | all-reduce | flops 512 | bytes 4096 | tf_op jit(solution)/shard_map/psum | solution.py:95
  897.8 43.6 %all-gather.8.cloned.1.call-done = f32[1,512,512]{2,1,0:T(8,128)} async-done(((f32[1,64,512]{2,1,0:T(8,128)}), f32[1,512,512]{2,1,0:T(8,128)}) %all-gather.8.cloned.1.call-update) | async-done | bytes 1048592 | tf_op jit(solution)/shard_map/all_gather | solution.py:71
  969.6 97.9 %all-reduce.8.cloned.1.call-done = (f32[4,128,512]{2,1,0:T(8,128)}, f32[4,128,512]{2,1,0:T(8,128)}) async-done(((f32[4,128,512]{2,1,0:T(8,128)}, f32[4,128,512]{2,1,0:T(8,128)}), (f32[4,128,512]{2,1,0:T(8,128)}, f32[4,128,512]{2,1,0:T(8,128)})) %all-reduce.8.cloned.1.call-update) | async-done | bytes 2097168 | tf_op jit(solution)/shard_map/psum | solution.py:12
  1084.7 46.0 %reduce-scatter.15.cloned.1.call-done = f32[2,8,1,4,512]{4,1,3,0,2:T(8,128)} async-done(((f32[2,8,16,4,512]{4,1,3,0,2:T(8,128)}), f32[2,8,1,4,512]{4,1,3,0,2:T(8,128)}) %reduce-scatter.15.cloned.1.call-update) | async-done | bytes 131088 | tf_op jit(solution)/shard_map/reduce_scatter | solution.py:81
  1131.8 13.3 %all_to_all.55 = f32[16,4,512]{2,1,0:T(4,128)S(1)} all-to-all(f32[16,4,512]{2,1,0:T(4,128)S(1)} %bitcast.99), channel_id=1, replica_groups=mesh['row'=8,'col'=16] {'row'}, dimensions={0} | all-to-all | bytes 262144 | tf_op jit(solution)/shard_map/all_to_all | solution.py:85
  1145.0 14.2 %all_to_all.56 = f32[16,4,512]{2,1,0:T(4,128)S(1)} all-to-all(f32[16,4,512]{2,1,0:T(4,128)S(1)} %all_to_all.55), channel_id=1, replica_groups=mesh['row'=8,'col'=16] {'col'}, dimensions={0} | all-to-all | bytes 262144 | tf_op jit(solution)/shard_map/all_to_all | solution.py:84
  1159.3 47.4 %reduce-scatter.17.cloned.1.call-done = f32[1,64,512]{2,1,0:T(8,128)} async-done(((f32[1,512,512]{2,1,0:T(8,128)}), f32[1,64,512]{2,1,0:T(8,128)}) %reduce-scatter.17.cloned.1.call-update) | async-done | bytes 131088 | tf_op jit(solution)/shard_map/reduce_scatter | solution.py:79
  1207.6 66.3 %psum.95 = f32[512]{0:T(512)S(1)} all-reduce(f32[512]{0:T(512)S(1)} %multiply_reduce_fusion), channel_id=1, replica_groups=mesh['row'=8,'col'=16] {'row','col'}, use_global_device_ids=true, to_apply=%region_23.25 | all-reduce | flops 512 | bytes 4096 | tf_op jit(solution)/shard_map/psum | solution.py:105
  (183 shorter events, 144.1 us)
Async XLA Ops:
  7.2 52.8 %all-gather.4.cloned.1.call-start = ((), (), s32[]{:S(2)}) async-start(), calls=%async_computation.12 | async-start | bytes 1179648 | tf_op jit(solution)/shard_map/all_gather | solution.py:71
  7.9 178.1 %all-reduce.12.cloned.1.call-start = ((), (), s32[]{:S(2)}) async-start(), calls=%async_computation.23 | async-start | bytes 4194304 | tf_op jit(solution)/shard_map/psum | solution.py:12
  62.9 186.4 %reduce-scatter.7.cloned.1.call-start = ((), (), s32[]{:S(2)}) async-start(), calls=%async_computation.13 | async-start | bytes 2228224 | tf_op jit(solution)/shard_map/reduce_scatter | solution.py:81
  63.7 444.2 %copy-start.22 = (pred[8]{0:T(512)(128)(4,1)}, pred[8]{0:T(512)(128)(4,1)S(1)}, u32[]{:S(2)}) copy-start(pred[8]{0:T(512)(128)(4,1)S(1)} %get-tuple-element.37) | copy-start | bytes 28
  63.7 454.0 %copy-start.20 = (pred[8]{0:T(512)(128)(4,1)}, pred[8]{0:T(512)(128)(4,1)S(1)}, u32[]{:S(2)}) copy-start(pred[8]{0:T(512)(128)(4,1)S(1)} %get-tuple-element.41) | copy-start | bytes 28
  63.7 567.9 %copy-start.18 = (pred[8]{0:T(512)(128)(4,1)}, pred[8]{0:T(512)(128)(4,1)S(1)}, u32[]{:S(2)}) copy-start(pred[8]{0:T(512)(128)(4,1)S(1)} %get-tuple-element.39) | copy-start | bytes 28
  63.7 573.8 %copy-start.16 = (pred[8]{0:T(512)(128)(4,1)}, pred[8]{0:T(512)(128)(4,1)S(1)}, u32[]{:S(2)}) copy-start(pred[8]{0:T(512)(128)(4,1)S(1)} %get-tuple-element.17) | copy-start | bytes 28
  63.7 440.0 %copy-start.36 = (s32[1024]{0:T(1024)}, s32[1024]{0:T(1024)S(1)}, u32[]{:S(2)}) copy-start(s32[1024]{0:T(1024)S(1)} %get-tuple-element.47) | copy-start | bytes 12292
  63.7 442.1 %copy-start.35 = (s32[1024]{0:T(1024)}, s32[1024]{0:T(1024)S(1)}, u32[]{:S(2)}) copy-start(s32[1024]{0:T(1024)S(1)} %get-tuple-element.48) | copy-start | bytes 12292
  63.8 447.8 %copy-start.31 = (s32[8]{0:T(128)}, s32[8]{0:T(128)S(1)}, u32[]{:S(2)}) copy-start(s32[8]{0:T(128)S(1)} %get-tuple-element.36) | copy-start | bytes 100
  63.8 455.9 %copy-start.29 = (s32[8]{0:T(128)}, s32[8]{0:T(128)S(1)}, u32[]{:S(2)}) copy-start(s32[8]{0:T(128)S(1)} %get-tuple-element.34) | copy-start | bytes 100
  63.8 571.5 %copy-start.27 = (s32[8]{0:T(128)}, s32[8]{0:T(128)S(1)}, u32[]{:S(2)}) copy-start(s32[8]{0:T(128)S(1)} %get-tuple-element.35) | copy-start | bytes 100
  63.8 575.9 %copy-start.24 = (s32[8]{0:T(128)}, s32[8]{0:T(128)S(1)}, u32[]{:S(2)}) copy-start(s32[8]{0:T(128)S(1)} %get-tuple-element.33) | copy-start | bytes 100
  87.2 238.0 %reduce-scatter.9.cloned.1.call-start = ((), (), s32[]{:S(2)}) async-start(), calls=%async_computation.14 | async-start | bytes 1179648 | tf_op jit(solution)/shard_map/reduce_scatter | solution.py:79
  87.5 539.0 %copy-start.34 = (s32[1024]{0:T(1024)}, s32[1024]{0:T(1024)S(1)}, u32[]{:S(2)}) copy-start(s32[1024]{0:T(1024)S(1)} %get-tuple-element.45) | copy-start | bytes 12292
  87.5 542.2 %copy-start.33 = (s32[1024]{0:T(1024)}, s32[1024]{0:T(1024)S(1)}, u32[]{:S(2)}) copy-start(s32[1024]{0:T(1024)S(1)} %get-tuple-element.46) | copy-start | bytes 12292
  202.9 297.4 %all-gather.6.cloned.1.call-start = ((), (), s32[]{:S(2)}) async-start(), calls=%async_computation.15 | async-start | bytes 1179648 | tf_op jit(solution)/shard_map/all_gather | solution.py:71
  456.7 169.7 %all-reduce.10.cloned.1.call-start = ((), (), s32[]{:S(2)}) async-start(), calls=%async_computation.22 | async-start | bytes 4194304 | tf_op jit(solution)/shard_map/psum | solution.py:12
  503.3 186.5 %reduce-scatter.11.cloned.1.call-start = ((), (), s32[]{:S(2)}) async-start(), calls=%async_computation.16 | async-start | bytes 2228224 | tf_op jit(solution)/shard_map/reduce_scatter | solution.py:81
  527.9 238.3 %reduce-scatter.13.cloned.1.call-start = ((), (), s32[]{:S(2)}) async-start(), calls=%async_computation.17 | async-start | bytes 1179648 | tf_op jit(solution)/shard_map/reduce_scatter | solution.py:79
  643.4 298.0 %all-gather.8.cloned.1.call-start = ((), (), s32[]{:S(2)}) async-start(), calls=%async_computation.18 | async-start | bytes 1179648 | tf_op jit(solution)/shard_map/all_gather | solution.py:71
  897.8 169.7 %all-reduce.8.cloned.1.call-start = ((), (), s32[]{:S(2)}) async-start(), calls=%async_computation.21 | async-start | bytes 4194304 | tf_op jit(solution)/shard_map/psum | solution.py:12
  944.4 186.4 %reduce-scatter.15.cloned.1.call-start = ((), (), s32[]{:S(2)}) async-start(), calls=%async_computation.19 | async-start | bytes 2228224 | tf_op jit(solution)/shard_map/reduce_scatter | solution.py:81
  969.4 237.3 %reduce-scatter.17.cloned.1.call-start = ((), (), s32[]{:S(2)}) async-start(), calls=%async_computation.20 | async-start | bytes 1179648 | tf_op jit(solution)/shard_map/reduce_scatter | solution.py:79
  (25 other events, 981.1 us)
Sparse Core Ops, SparseCore 0:
  10.3 49.5 all-gather.3
  63.0 122.9 all-reduce.11
  188.4 60.8 reduce-scatter.6
  252.8 72.3 reduce-scatter.8
  456.8 43.4 all-gather.5
  503.4 122.9 all-reduce.9
  628.9 60.8 reduce-scatter.10
  693.9 72.3 reduce-scatter.12
  897.9 43.4 all-gather.7
  944.5 122.9 all-reduce.7
  1069.9 60.8 reduce-scatter.14
  1134.3 72.3 reduce-scatter.16
where the time goes:
time: 1290 us; the launch traced here: 1280 us
  waiting for transfers between devices  714 us (55%)
  blocking collectives  407 us (32%)
  matrix products  62.8 us (5%)
  local copies, waits for them, and re-layouts  59.1 us (5%)
  other arithmetic  23.3 us (2%)
  between operations  15.1 us (1%)
    psum x3, waiting for transfers between devices, broadcast(): return lax.psum(kept, axis)  295 us
    psum x3, blocking collectives, squares(): return lax.psum(jnp.sum(residual * residual, axis=(0, 1)), ('row', 'col'))  191 us
    reduce_scatter x3, waiting for transfers between devices, operate(): lax.psum_scatter(backward[None], 'row', scatter_dimension=1, tiled=True)  142 us
    reduce_scatter x3, waiting for transfers between devices, operate(): summed = lax.psum_scatter(spread, 'col', scatter_dimension=2, tiled=True)  139 us
    all_gather x3, waiting for transfers between devices, operate(): whole = lax.all_gather(piece, 'row', axis=1, tiled=True)  137 us
    psum x2, blocking collectives, shards(): curve = lax.psum(jnp.sum(direction * image, axis=(0, 1)), ('row', 'col'))  133 us
    all_to_all x3, blocking collectives, operate(): lax.all_to_all(lax.all_to_all(ordered, 'row', split_axis=0, concat_axis=0...  42.7 us
    all_to_all x3, blocking collectives, operate(): lax.all_to_all(ordered, 'row', split_axis=0, concat_axis=0, tiled=True)  39.9 us
  transfers between devices with their start and end apart: 12, of which 12 were waited for; matrix products, arithmetic and copies ran while one was open for 10% of the time, Pallas kernels for 0%

commit v1 on v0

--- a/solution.py
+++ b/solution.py
@@ -81,12 +81,20 @@
     summed = lax.psum_scatter(spread, "col", scatter_dimension=2, tiled=True)
     ordered = summed.reshape(members, rows_count, sliver, width).transpose(1, 0, 2, 3)
     ordered = ordered.reshape(rows_count * members, sliver, width)
-    forward_part = lax.all_to_all(
-        lax.all_to_all(ordered, "row", split_axis=0, concat_axis=0, tiled=True),
-        "col",
-        split_axis=0,
-        concat_axis=1,
-        tiled=True,
+    forward_part = jnp.concatenate(
+        lax.all_to_all(
+            jnp.stack(
+                jnp.split(
+                    lax.all_to_all(ordered, "row", split_axis=0, concat_axis=0, tiled=True),
+                    lax.axis_size("col"),
+                    axis=0,
+                )
+            ),
+            "col",
+            0,
+            0,
+        ),
+        axis=1,
     )
     return piece - diffusion * (forward_part + back_part)
 

time: 1290 us -> 1330 us (1.031)
  blocking collectives: 407 us -> 367 us
  waiting for transfers between devices: 714 us -> 749 us
  starting transfers between devices: 1.83 us -> 20.5 us
  local copies, waits for them, and re-layouts: 59.1 us -> 74.1 us
    all_to_all x6 -> x3, blocking collectives: 82.6 us -> 43 us  [operate(): lax.all_to_all(jnp.stack(jnp.split(lax.all_to_all(ordered, 'row', split_a...]
    all_to_all x0 -> x3, starting transfers between devices: none -> 19.6 us  [operate(): lax.all_to_all(ordered, 'row', split_axis=0, concat_axis=0, tiled=True)]
    reduce_scatter x3, waiting for transfers between devices: 142 us -> 159 us  [operate(): lax.psum_scatter(backward[None], 'row', scatter_dimension=1, tiled=True)]
  transfers between devices with their start and end apart: 12 -> 15, of which waited for: 12 -> 15; matrix products, arithmetic and copies ran while one was open for 10% -> 11% of each run, Pallas kernels for 0% -> 0%
where the time goes in v1:
time: 1330 us; the launch traced here: 1310 us
  waiting for transfers between devices  749 us (56%)
  blocking collectives  367 us (28%)
  local copies, waits for them, and re-layouts  74.1 us (6%)
  matrix products  64.6 us (5%)
  other arithmetic  23.4 us (2%)
  starting transfers between devices  20.5 us (2%)
  between operations  15.5 us (1%)
    psum x3, waiting for transfers between devices, broadcast(): return lax.psum(kept, axis)  295 us
    psum x3, blocking collectives, squares(): return lax.psum(jnp.sum(residual * residual, axis=(0, 1)), ('row', 'col'))  191 us
    reduce_scatter x3, waiting for transfers between devices, operate(): lax.psum_scatter(backward[None], 'row', scatter_dimension=1, tiled=True)  159 us
    reduce_scatter x3, waiting for transfers between devices, operate(): summed = lax.psum_scatter(spread, 'col', scatter_dimension=2, tiled=True)  150 us
    all_gather x3, waiting for transfers between devices, operate(): whole = lax.all_gather(piece, 'row', axis=1, tiled=True)  137 us
    psum x2, blocking collectives, shards(): curve = lax.psum(jnp.sum(direction * image, axis=(0, 1)), ('row', 'col'))  133 us
    all_to_all x3, blocking collectives, operate(): lax.all_to_all(jnp.stack(jnp.split(lax.all_to_all(ordered, 'row', split_a...  43 us
  transfers between devices with their start and end apart: 15, of which 15 were waited for; matrix products, arithmetic and copies ran while one was open for 11% of the time, Pallas kernels for 0%

profile of v1, /device:TPU:1, one launch (start us, length us, event | category | flops | bytes accessed | tf_op | source)
XLA Modules:
  0.0 1313.8 jit_solution(4854405425362829065)
XLA Ops:
  9.9 50.0 %all-gather.4.cloned.1.call-done = f32[1,512,512]{2,1,0:T(8,128)} async-done(((f32[1,64,512]{2,1,0:T(8,128)}), f32[1,512,512]{2,1,0:T(8,128)}) %all-gather.4.cloned.1.call-update) | async-done | bytes 1048592 | tf_op jit(solution)/shard_map/all_gather | solution.py:71
  75.4 3.6 fusion.46
  87.3 98.7 %all-reduce.12.cloned.1.call-done = (f32[4,128,512]{2,1,0:T(8,128)}, f32[4,128,512]{2,1,0:T(8,128)}) async-done(((f32[4,128,512]{2,1,0:T(8,128)}, f32[4,128,512]{2,1,0:T(8,128)}), (f32[4,128,512]{2,1,0:T(8,128)}, f32[4,128,512]{2,1,0:T(8,128)})) %all-reduce.12.cloned.1.call-update) | async-done | bytes 2097168 | tf_op jit(solution)/shard_map/psum | solution.py:12
  199.1 50.2 %reduce-scatter.7.cloned.1.call-done = f32[2,8,1,4,512]{4,1,3,0,2:T(8,128)} async-done(((f32[2,8,16,4,512]{4,1,3,0,2:T(8,128)}), f32[2,8,1,4,512]{4,1,3,0,2:T(8,128)}) %reduce-scatter.7.cloned.1.call-update) | async-done | bytes 131088 | tf_op jit(solution)/shard_map/reduce_scatter | solution.py:81
  251.0 6.5 all-to-all-start
  264.6 14.3 %all_to_all.30 = f32[16,1,4,512]{3,2,1,0:T(4,128)S(1)} all-to-all(f32[16,1,4,512]{3,2,1,0:T(4,128)S(1)} %constant_dynamic-update-slice_fusion), channel_id=1, replica_groups=mesh['row'=8,'col'=16] {'col'}, dimensions={0} | all-to-all | bytes 262144 | tf_op jit(solution)/shard_map/all_to_all | solution.py:85
  279.0 56.7 %reduce-scatter.9.cloned.1.call-done = f32[1,64,512]{2,1,0:T(8,128)} async-done(((f32[1,512,512]{2,1,0:T(8,128)}), f32[1,64,512]{2,1,0:T(8,128)}) %reduce-scatter.9.cloned.1.call-update) | async-done | bytes 131088 | tf_op jit(solution)/shard_map/reduce_scatter | solution.py:79
  336.7 66.3 %all-reduce = (f32[512]{0:T(512)S(1)}, f32[512]{0:T(512)S(1)}) all-reduce(f32[512]{0:T(512)S(1)} %get-tuple-element.4, f32[512]{0:T(512)S(1)} %get-tuple-element.3), channel_id=1, replica_groups=mesh['row'=8,'col'=16] {'row','col'}, use_global_device_ids=true, to_apply=%region_1.0 | all-reduce | flops 1024 | bytes 8192 | tf_op jit(solution)/shard_map/psum | solution.py:103
  404.0 62.5 %psum.88 = f32[512]{0:T(512)S(1)} all-reduce(f32[512]{0:T(512)S(1)} %get-tuple-element.15), channel_id=1, replica_groups=mesh['row'=8,'col'=16] {'row','col'}, use_global_device_ids=true, to_apply=%region_9.11 | all-reduce | flops 512 | bytes 4096 | tf_op jit(solution)/shard_map/psum | solution.py:103
  467.3 43.6 %all-gather.6.cloned.1.call-done = f32[1,512,512]{2,1,0:T(8,128)} async-done(((f32[1,64,512]{2,1,0:T(8,128)}), f32[1,512,512]{2,1,0:T(8,128)}) %all-gather.6.cloned.1.call-update) | async-done | bytes 1048592 | tf_op jit(solution)/shard_map/all_gather | solution.py:71
  538.7 98.3 %all-reduce.10.cloned.1.call-done = (f32[4,128,512]{2,1,0:T(8,128)}, f32[4,128,512]{2,1,0:T(8,128)}) async-done(((f32[4,128,512]{2,1,0:T(8,128)}, f32[4,128,512]{2,1,0:T(8,128)}), (f32[4,128,512]{2,1,0:T(8,128)}, f32[4,128,512]{2,1,0:T(8,128)})) %all-reduce.10.cloned.1.call-update) | async-done | bytes 2097168 | tf_op jit(solution)/shard_map/psum | solution.py:12
  650.3 50.0 %reduce-scatter.11.cloned.1.call-done = f32[2,8,1,4,512]{4,1,3,0,2:T(8,128)} async-done(((f32[2,8,16,4,512]{4,1,3,0,2:T(8,128)}), f32[2,8,1,4,512]{4,1,3,0,2:T(8,128)}) %reduce-scatter.11.cloned.1.call-update) | async-done | bytes 131088 | tf_op jit(solution)/shard_map/reduce_scatter | solution.py:81
  702.0 6.6 all-to-all-start.2
  726.9 14.4 %all_to_all.31 = f32[16,1,4,512]{3,2,1,0:T(4,128)S(1)} all-to-all(f32[16,1,4,512]{3,2,1,0:T(4,128)S(1)} %constant_dynamic-update-slice_fusion.16), channel_id=1, replica_groups=mesh['row'=8,'col'=16] {'col'}, dimensions={0} | all-to-all | bytes 262144 | tf_op jit(solution)/shard_map/all_to_all | solution.py:85
  741.4 45.2 %reduce-scatter.13.cloned.1.call-done = f32[1,64,512]{2,1,0:T(8,128)} async-done(((f32[1,512,512]{2,1,0:T(8,128)}), f32[1,64,512]{2,1,0:T(8,128)}) %reduce-scatter.13.cloned.1.call-update) | async-done | bytes 131088 | tf_op jit(solution)/shard_map/reduce_scatter | solution.py:79
  787.5 66.3 %psum.91 = f32[512]{0:T(512)S(1)} all-reduce(f32[512]{0:T(512)S(1)} %multiply_reduce_fusion.2), channel_id=1, replica_groups=mesh['row'=8,'col'=16] {'row','col'}, use_global_device_ids=true, to_apply=%region_15.17 | all-reduce | flops 512 | bytes 4096 | tf_op jit(solution)/shard_map/psum | solution.py:113
  854.8 62.6 %psum.92 = f32[512]{0:T(512)S(1)} all-reduce(f32[512]{0:T(512)S(1)} %get-tuple-element.13), channel_id=1, replica_groups=mesh['row'=8,'col'=16] {'row','col'}, use_global_device_ids=true, to_apply=%region_17.19 | all-reduce | flops 512 | bytes 4096 | tf_op jit(solution)/shard_map/psum | solution.py:103
  918.1 43.7 %all-gather.8.cloned.1.call-done = f32[1,512,512]{2,1,0:T(8,128)} async-done(((f32[1,64,512]{2,1,0:T(8,128)}), f32[1,512,512]{2,1,0:T(8,128)}) %all-gather.8.cloned.1.call-update) | async-done | bytes 1048592 | tf_op jit(solution)/shard_map/all_gather | solution.py:71
  989.6 98.4 %all-reduce.8.cloned.1.call-done = (f32[4,128,512]{2,1,0:T(8,128)}, f32[4,128,512]{2,1,0:T(8,128)}) async-done(((f32[4,128,512]{2,1,0:T(8,128)}, f32[4,128,512]{2,1,0:T(8,128)}), (f32[4,128,512]{2,1,0:T(8,128)}, f32[4,128,512]{2,1,0:T(8,128)})) %all-reduce.8.cloned.1.call-update) | async-done | bytes 2097168 | tf_op jit(solution)/shard_map/psum | solution.py:12
  1101.1 50.1 %reduce-scatter.15.cloned.1.call-done = f32[2,8,1,4,512]{4,1,3,0,2:T(8,128)} async-done(((f32[2,8,16,4,512]{4,1,3,0,2:T(8,128)}), f32[2,8,1,4,512]{4,1,3,0,2:T(8,128)}) %reduce-scatter.15.cloned.1.call-update) | async-done | bytes 131088 | tf_op jit(solution)/shard_map/reduce_scatter | solution.py:81
  1152.9 6.6 all-to-all-start.4
  1166.5 14.2 %all_to_all.32 = f32[16,1,4,512]{3,2,1,0:T(4,128)S(1)} all-to-all(f32[16,1,4,512]{3,2,1,0:T(4,128)S(1)} %constant_dynamic-update-slice_fusion.32), channel_id=1, replica_groups=mesh['row'=8,'col'=16] {'col'}, dimensions={0} | all-to-all | bytes 262144 | tf_op jit(solution)/shard_map/all_to_all | solution.py:85
  1180.8 56.8 %reduce-scatter.17.cloned.1.call-done = f32[1,64,512]{2,1,0:T(8,128)} async-done(((f32[1,512,512]{2,1,0:T(8,128)}), f32[1,64,512]{2,1,0:T(8,128)}) %reduce-scatter.17.cloned.1.call-update) | async-done | bytes 131088 | tf_op jit(solution)/shard_map/reduce_scatter | solution.py:79
  1238.5 66.3 %psum.95 = f32[512]{0:T(512)S(1)} all-reduce(f32[512]{0:T(512)S(1)} %multiply_reduce_fusion), channel_id=1, replica_groups=mesh['row'=8,'col'=16] {'row','col'}, use_global_device_ids=true, to_apply=%region_23.25 | all-reduce | flops 512 | bytes 4096 | tf_op jit(solution)/shard_map/psum | solution.py:113
  (260 shorter events, 166.2 us)
Async XLA Ops:
  7.2 52.8 %all-gather.4.cloned.1.call-start = ((), (), s32[]{:S(2)}) async-start(), calls=%async_computation.12 | async-start | bytes 1179648 | tf_op jit(solution)/shard_map/all_gather | solution.py:71
  7.9 178.2 %all-reduce.12.cloned.1.call-start = ((), (), s32[]{:S(2)}) async-start(), calls=%async_computation.23 | async-start | bytes 4194304 | tf_op jit(solution)/shard_map/psum | solution.py:12
  63.0 186.4 %reduce-scatter.7.cloned.1.call-start = ((), (), s32[]{:S(2)}) async-start(), calls=%async_computation.13 | async-start | bytes 2228224 | tf_op jit(solution)/shard_map/reduce_scatter | solution.py:81
  63.7 127.8 %copy-start.24 = (pred[8]{0:T(512)(128)(4,1)}, pred[8]{0:T(512)(128)(4,1)S(1)}, u32[]{:S(2)}) copy-start(pred[8]{0:T(512)(128)(4,1)S(1)} %get-tuple-element.39) | copy-start | bytes 28
  63.7 133.2 %copy-start.21 = (pred[8]{0:T(512)(128)(4,1)}, pred[8]{0:T(512)(128)(4,1)S(1)}, u32[]{:S(2)}) copy-start(pred[8]{0:T(512)(128)(4,1)S(1)} %get-tuple-element.17) | copy-start | bytes 28
  63.8 129.9 %copy-start.37 = (s32[8]{0:T(128)}, s32[8]{0:T(128)S(1)}, u32[]{:S(2)}) copy-start(s32[8]{0:T(128)S(1)} %get-tuple-element.35) | copy-start | bytes 100
  63.8 193.7 %copy-start.33 = (s32[8]{0:T(128)}, s32[8]{0:T(128)S(1)}, u32[]{:S(2)}) copy-start(s32[8]{0:T(128)S(1)} %get-tuple-element.33) | copy-start | bytes 100
  87.3 101.0 %copy-start.47 = (s32[1024]{0:T(1024)}, s32[1024]{0:T(1024)S(1)}, u32[]{:S(2)}) copy-start(s32[1024]{0:T(1024)S(1)} %get-tuple-element.45) | copy-start | bytes 12292
  87.3 101.0 %copy-start.46 = (s32[1024]{0:T(1024)}, s32[1024]{0:T(1024)S(1)}, u32[]{:S(2)}) copy-start(s32[1024]{0:T(1024)S(1)} %get-tuple-element.46) | copy-start | bytes 12292
  251.0 13.4 %all-to-all-start = ((f32[16,4,512]{2,1,0:T(4,128)}), f32[16,4,512]{2,1,0:T(4,128)S(1)}, u32[]{:S(2)}, u32[]{:S(2)}) async-start(f32[16,4,512]{2,1,0:T(4,128)} %bitcast.13), calls=%async_computation.1 | async-start | bytes 262144 | tf_op jit(solution)/shard_map/all_to_all | solution.py:88
  257.5 78.2 %reduce-scatter.9.cloned.1.call-start = ((), (), s32[]{:S(2)}) async-start(), calls=%async_computation.14 | async-start | bytes 1179648 | tf_op jit(solution)/shard_map/reduce_scatter | solution.py:79
  262.4 248.5 %all-gather.6.cloned.1.call-start = ((), (), s32[]{:S(2)}) async-start(), calls=%async_computation.15 | async-start | bytes 1179648 | tf_op jit(solution)/shard_map/all_gather | solution.py:71
  467.2 169.8 %all-reduce.10.cloned.1.call-start = ((), (), s32[]{:S(2)}) async-start(), calls=%async_computation.22 | async-start | bytes 4194304 | tf_op jit(solution)/shard_map/psum | solution.py:12
  513.9 186.5 %reduce-scatter.11.cloned.1.call-start = ((), (), s32[]{:S(2)}) async-start(), calls=%async_computation.16 | async-start | bytes 2228224 | tf_op jit(solution)/shard_map/reduce_scatter | solution.py:81
  702.0 13.6 %all-to-all-start.2 = ((f32[16,4,512]{2,1,0:T(4,128)}), f32[16,4,512]{2,1,0:T(4,128)}, u32[]{:S(2)}, u32[]{:S(2)}) async-start(f32[16,4,512]{2,1,0:T(4,128)} %bitcast.38), calls=%async_computation.5 | async-start | bytes 262144 | tf_op jit(solution)/shard_map/all_to_all | solution.py:88
  708.6 78.0 %reduce-scatter.13.cloned.1.call-start = ((), (), s32[]{:S(2)}) async-start(), calls=%async_computation.17 | async-start | bytes 1179648 | tf_op jit(solution)/shard_map/reduce_scatter | solution.py:79
  713.5 248.4 %all-gather.8.cloned.1.call-start = ((), (), s32[]{:S(2)}) async-start(), calls=%async_computation.18 | async-start | bytes 1179648 | tf_op jit(solution)/shard_map/all_gather | solution.py:71
  918.1 169.9 %all-reduce.8.cloned.1.call-start = ((), (), s32[]{:S(2)}) async-start(), calls=%async_computation.21 | async-start | bytes 4194304 | tf_op jit(solution)/shard_map/psum | solution.py:12
  964.9 186.4 %reduce-scatter.15.cloned.1.call-start = ((), (), s32[]{:S(2)}) async-start(), calls=%async_computation.19 | async-start | bytes 2228224 | tf_op jit(solution)/shard_map/reduce_scatter | solution.py:81
  1152.9 13.5 %all-to-all-start.4 = ((f32[16,4,512]{2,1,0:T(4,128)}), f32[16,4,512]{2,1,0:T(4,128)S(1)}, u32[]{:S(2)}, u32[]{:S(2)}) async-start(f32[16,4,512]{2,1,0:T(4,128)} %bitcast.61), calls=%async_computation.9 | async-start | bytes 262144 | tf_op jit(solution)/shard_map/all_to_all | solution.py:88
  1159.4 78.1 %reduce-scatter.17.cloned.1.call-start = ((), (), s32[]{:S(2)}) async-start(), calls=%async_computation.20 | async-start | bytes 1179648 | tf_op jit(solution)/shard_map/reduce_scatter | solution.py:79
  1163.0 141.9 %copy-start.20 = (f32[512]{0:T(512)S(1)}, f32[512]{0:T(512)}, u32[]{:S(2)}) copy-start(f32[512]{0:T(512)} %copy-done.19) | copy-start | bytes 6148
  1163.0 141.9 %copy-start.16 = (f32[1,64,512]{2,1,0:T(8,128)S(1)}, f32[1,64,512]{2,1,0:T(8,128)}, u32[]{:S(2)}) copy-start(f32[1,64,512]{2,1,0:T(8,128)} %copy-done.15) | copy-start | bytes 393220
  1163.0 141.9 %copy-start.18 = (f32[512]{0:T(512)S(1)}, f32[512]{0:T(512)}, u32[]{:S(2)}) copy-start(f32[512]{0:T(512)} %copy-done.17) | copy-start | bytes 6148
  (41 other events, 649.8 us)
Sparse Core Ops, SparseCore 0:
  10.3 49.5 all-gather.3
  63.1 122.9 all-reduce.11
  188.5 60.8 reduce-scatter.6
  262.5 73.1 reduce-scatter.8
  467.3 43.4 all-gather.5
  514.0 122.9 all-reduce.9
  639.5 60.8 reduce-scatter.10
  713.6 72.9 reduce-scatter.12
  918.2 43.6 all-gather.7
  965.0 122.9 all-reduce.7
  1090.4 60.8 reduce-scatter.14
  1164.5 73.0 reduce-scatter.16
